TPU v7x, 32 devices: a whole 2x2x4 slice. The times are simulated.
32 devices in a mesh: patch: 8 (over z, x), grp: 4 (over y, core).
Axes of the slice: x: 2, y: 2, z: 4, core: 2. Of those that a mesh axis runs over, the one named last changes fastest.
Arguments:
- previous: float32 [4, 8, 12, 21, 256], P('grp', 'patch'), may hold values from -4 to 4
- predicted: float32 [4, 8, 12, 21, 256], P('grp', 'patch'), may hold values from -4 to 4
- new_owner: int32 [4, 8, 12], replicated, may hold values from 0 to 7, as said below
- levels: int32 [4, 8, 12], replicated, may hold values from 0 to 2
- diffusion: float32 [21], replicated, may hold values from 0.05 to 0.5
- decay: float32 [21], replicated, may hold values from 0.1 to 1
- reaction: float32 [21, 21], replicated, may hold values from -1.25 to 1.25
Outputs:
- solution: float32 [4, 8, 16, 21, 256], P('grp', 'patch')
Inputs may be any that keep to these rules, and one draw needn't show every extreme that they name: new_owner[b, o, s] is o, except that a patch of the last column of an owner o < 7 may get o + 1 and a patch of the first column of an owner o > 0 may get o - 1; at most 2 patches of one owner get o + 1 and at most 2 get o - 1; owner (0, 0) hands exactly 2 to o + 1 and owner (0, 7) exactly 2 to o - 1.
All inputs are finite; a program needn't handle non-finite values.
Results may differ from a plain program's by a relative error of at most 0.0003.
Values sent between devices are 32-bit elements; how exact they have to be, the bound alone decides.
A program may use at most 128 MiB of HBM per device.

v0:
```python
import jax
import jax.numpy as jnp
from jax import lax
from jax.sharding import PartitionSpec as P

SPECIES = 21
CELLS = 16
ROWS_DEV = 4
COLS_DEV = 3
MOVE_CAP = 2
KRYLOV = 3
NEWTON = 2
PATCH_DEV = 12


step_rate = 4.0
epsilon = 1e-12
highest = lax.Precision.HIGHEST
opposite = (1, 0, 3, 2)


def extended(x, sides, width):
    for axis, dim in sides:
        devices, length = (lax.axis_size(axis), x.shape[dim])
        up = [(i, (i + 1) % devices) for i in range(devices - 1)]
        down = [(j, i) for i, j in up]
        last = lax.slice_in_dim(x, length - width, length, axis=dim)
        initial = lax.slice_in_dim(x, 0, width, axis=dim)
        before = lax.ppermute(last, axis, up)
        after = lax.ppermute(initial, axis, down)
        x = jnp.concatenate([before, x, after], axis=dim)
    return x


def passed_along(block, axis, distance):
    devices = range(lax.axis_size(axis))
    route = [(i - distance, i) for i in devices if i - distance in devices]
    return lax.ppermute(block, axis, route)


def slot_layout(new_owner, device_rows, capacity):
    band_total, owner_total, patch_count = new_owner.shape
    device_cols = patch_count // device_rows
    owner_line = jnp.arange(owner_total, dtype=jnp.int32)[None, :, None]
    offset = new_owner - owner_line
    patch_ids = jnp.arange(band_total * owner_total * patch_count, dtype=jnp.int32).reshape(
        band_total, owner_total, patch_count
    )
    staying = jnp.where(offset == 0, patch_ids, -1)
    grid_ids = patch_ids.reshape(band_total, owner_total, device_rows, device_cols)
    grid_off = offset.reshape(band_total, owner_total, device_rows, device_cols)

    def packed(column_at, sign):
        moving = (grid_off[:, :, :, column_at] == sign).astype(jnp.int32)
        ranks = jnp.cumsum(moving, axis=-1) - 1
        choose = (moving[..., None] == 1) & (
            ranks[..., None] == jnp.arange(capacity, dtype=jnp.int32)
        )
        present = jnp.any(choose, axis=2)
        summed = jnp.sum(jnp.where(choose, grid_ids[:, :, :, column_at][..., None], 0), axis=2)
        return jnp.where(present, summed, -1)

    rightward = packed(device_cols - 1, 1)
    leftward = packed(0, -1)
    filler = jnp.full((band_total, 1, capacity), -1, jnp.int32)
    from_left = jnp.concatenate([filler, rightward[:, :-1]], axis=1)
    from_right = jnp.concatenate([leftward[:, 1:], filler], axis=1)
    return jnp.concatenate([staying, from_left, from_right], axis=2)


def neighbor_ids(patch_ids, band_total, owner_total):
    valid = patch_ids >= 0
    safe = jnp.maximum(patch_ids, 0)
    per_owner = ROWS_DEV * COLS_DEV
    column_of = safe % COLS_DEV
    row_of = safe // COLS_DEV % ROWS_DEV
    owner_of = safe // per_owner % owner_total
    band_of = safe // (per_owner * owner_total)

    def compose(band_val, owner_val, row_val, column_val, inside):
        ident = ((band_val * owner_total + owner_val) * ROWS_DEV + row_val) * COLS_DEV + column_val
        return jnp.where(inside & valid, ident, -1)

    west = compose(
        band_of,
        jnp.where(column_of > 0, owner_of, owner_of - 1),
        row_of,
        jnp.where(column_of > 0, column_of - 1, COLS_DEV - 1),
        (column_of > 0) | (owner_of > 0),
    )
    east = compose(
        band_of,
        jnp.where(column_of < COLS_DEV - 1, owner_of, owner_of + 1),
        row_of,
        jnp.where(column_of < COLS_DEV - 1, column_of + 1, 0),
        (column_of < COLS_DEV - 1) | (owner_of < owner_total - 1),
    )
    south = compose(
        jnp.where(row_of > 0, band_of, band_of - 1),
        owner_of,
        jnp.where(row_of > 0, row_of - 1, ROWS_DEV - 1),
        column_of,
        (row_of > 0) | (band_of > 0),
    )
    north = compose(
        jnp.where(row_of < ROWS_DEV - 1, band_of, band_of + 1),
        owner_of,
        jnp.where(row_of < ROWS_DEV - 1, row_of + 1, 0),
        column_of,
        (row_of < ROWS_DEV - 1) | (band_of < band_total - 1),
    )
    return jnp.stack([west, east, south, north], axis=-1)


def conductance(level_vals):
    return jnp.where(level_vals == 0, 1.0, jnp.where(level_vals == 1, 4.0, 16.0)).astype(
        jnp.float32
    )


def small_solve(gram, rhs):
    dimension = gram.shape[0]
    matrix = gram
    vector = rhs
    for column_at in range(dimension):
        for target in range(column_at + 1, dimension):
            factor = matrix[target, column_at] / matrix[column_at, column_at]
            matrix = matrix.at[target].add(-factor * matrix[column_at])
            vector = vector.at[target].add(-factor * vector[column_at])
    answer = [None] * dimension
    for column_at in reversed(range(dimension)):
        running = vector[column_at]
        for later in range(column_at + 1, dimension):
            running = running - matrix[column_at, later] * answer[later]
        answer[column_at] = running / matrix[column_at, column_at]
    return jnp.stack(answer)


def pack_movers(offset, data):
    grid_off = offset.reshape(ROWS_DEV, COLS_DEV)
    row_slots = jnp.arange(ROWS_DEV, dtype=jnp.int32) * COLS_DEV
    packs = []
    for column_at, sign in ((COLS_DEV - 1, 1), (0, -1)):
        moving = (grid_off[:, column_at] == sign).astype(jnp.int32)
        ranks = jnp.cumsum(moving) - 1
        choose = (moving[:, None] == 1) & (
            ranks[:, None] == jnp.arange(MOVE_CAP, dtype=jnp.int32)[None, :]
        )
        present = jnp.any(choose, axis=0)
        source = jnp.sum(jnp.where(choose, (row_slots + column_at)[:, None], 0), axis=0)
        picked = jnp.take(data, source, axis=0)
        packs.append(jnp.where(present.reshape((MOVE_CAP,) + (1,) * (data.ndim - 1)), picked, 0.0))
    return packs


def neighbor_strips(values, window_tags, near_ids):
    slot_count = values.shape[0]
    squared = values.reshape(slot_count, SPECIES, CELLS, CELLS)
    bank = jnp.stack(
        [squared[:, :, :, 0], squared[:, :, :, -1], squared[:, :, 0, :], squared[:, :, -1, :]],
        axis=0,
    )
    flat = bank.reshape(1, 1, -1)
    received = extended(flat, (("patch", 1), ("grp", 0)), 1)
    pieces = received.reshape(9, 4, slot_count, SPECIES * CELLS)
    tags = window_tags.reshape(9 * slot_count)
    ghosts = []
    for direction in range(4):
        wanted = near_ids[:, direction]
        selector = ((wanted[:, None] == tags[None, :]) & (wanted[:, None] >= 0)).astype(jnp.float32)
        candidates = pieces[:, opposite[direction]].reshape(9 * slot_count, SPECIES * CELLS)
        picked = jnp.dot(
            selector, candidates, precision=highest, preferred_element_type=jnp.float32
        )
        ghosts.append(picked.reshape(slot_count, SPECIES, CELLS))
    return ghosts


def laplace_slots(values, ghosts, face_self, face_near):
    slot_count = values.shape[0]
    flat_pos = jnp.arange(CELLS * CELLS, dtype=jnp.int32)
    column_of = flat_pos % CELLS
    row_of = flat_pos // CELLS
    zero_one = jnp.zeros((slot_count, SPECIES, 1), jnp.float32)
    zero_row = jnp.zeros((slot_count, SPECIES, CELLS), jnp.float32)
    west_vals = jnp.where(
        column_of == 0,
        jnp.repeat(ghosts[0], CELLS, axis=-1),
        jnp.concatenate([zero_one, values[:, :, :-1]], axis=2),
    )
    east_vals = jnp.where(
        column_of == CELLS - 1,
        jnp.repeat(ghosts[1], CELLS, axis=-1),
        jnp.concatenate([values[:, :, 1:], zero_one], axis=2),
    )
    south_vals = jnp.where(
        row_of == 0,
        jnp.tile(ghosts[2], (1, 1, CELLS)),
        jnp.concatenate([zero_row, values[:, :, :-CELLS]], axis=2),
    )
    north_vals = jnp.where(
        row_of == CELLS - 1,
        jnp.tile(ghosts[3], (1, 1, CELLS)),
        jnp.concatenate([values[:, :, CELLS:], zero_row], axis=2),
    )
    own_face = face_self[:, None, None]

    def face(edge_mask, direction):
        return jnp.where(
            edge_mask,
            0.5 * (own_face + face_near[:, direction][:, None, None]),
            0.5 * (own_face + own_face),
        )

    return (
        face(column_of == 0, 0) * (west_vals - values)
        + face(column_of == CELLS - 1, 1) * (east_vals - values)
        + face(row_of == 0, 2) * (south_vals - values)
        + face(row_of == CELLS - 1, 3) * (north_vals - values)
    )


def newton_solve(
    prev_slots, pred_slots, layout_ids, band_pos, owner_pos, levels, diffusion, decay, reaction
):
    band_total, owner_total, slot_count = layout_ids.shape
    slot_ids = lax.dynamic_slice(layout_ids, (band_pos, owner_pos, 0), (1, 1, slot_count))[0, 0]
    padded_ids = jnp.pad(layout_ids, ((1, 1), (1, 1), (0, 0)), constant_values=-1)
    window_tags = lax.dynamic_slice(padded_ids, (band_pos, owner_pos, 0), (3, 3, slot_count))
    near_ids = neighbor_ids(slot_ids, band_total, owner_total)
    level_flat = levels.reshape(-1)

    def kappa_of(ident):
        return jnp.where(ident >= 0, conductance(jnp.take(level_flat, jnp.maximum(ident, 0))), 0.0)

    face_self = kappa_of(slot_ids)
    face_near = jnp.where(near_ids >= 0, kappa_of(near_ids), face_self[:, None])
    differential = (jnp.arange(SPECIES) < SPECIES - 1).astype(jnp.float32)[None, :, None]
    diff_col = diffusion[None, :, None]
    decay_col = decay[None, :, None]

    def laplace_of(values):
        return laplace_slots(
            values, neighbor_strips(values, window_tags, near_ids), face_self, face_near
        )

    def mixing(values):
        return jnp.einsum("st,kta->ksa", reaction, values, precision=highest)

    state = pred_slots
    for newton_step in range(NEWTON):
        resid = (
            differential * step_rate * (state - prev_slots)
            - diff_col * laplace_of(state)
            - mixing(state)
            + decay_col * (state * state * state)
        )
        squares = lax.psum(jnp.sum(resid * resid), ("patch", "grp"))
        scale = jnp.sqrt(squares + epsilon)
        basis = [-resid / scale]
        curvature = 3.0 * decay_col * (state * state)
        hess = jnp.zeros((KRYLOV + 1, KRYLOV), jnp.float32)
        for column_at in range(KRYLOV):
            current = basis[column_at]
            image = (
                differential * step_rate * current
                - diff_col * laplace_of(current)
                - mixing(current)
                + curvature * current
            )
            stacked = jnp.stack(basis)
            local_products = jnp.einsum("mksa,ksa->m", stacked, image, precision=highest)
            coeffs, length_sq = lax.psum((local_products, jnp.sum(image * image)), ("patch", "grp"))
            image = image - jnp.einsum("m,mksa->ksa", coeffs, stacked, precision=highest)
            height = jnp.sqrt(length_sq - jnp.sum(coeffs * coeffs) + epsilon)
            hess = hess.at[: column_at + 1, column_at].set(coeffs)
            hess = hess.at[column_at + 1, column_at].set(height)
            basis.append(image / height)
        gram = jnp.dot(hess.T, hess, precision=highest)
        weights = small_solve(gram, scale * hess[0])
        state = state + jnp.einsum(
            "m,mksa->ksa", weights, jnp.stack(basis[:KRYLOV]), precision=highest
        )
    return state


def per_device(previous, predicted, new_owner, levels, diffusion, decay, reaction):
    band_pos = lax.axis_index("grp")
    owner_pos = lax.axis_index("patch")
    previous = previous[0, 0]
    predicted = predicted[0, 0]
    own_offset = (
        lax.dynamic_slice(new_owner, (band_pos, owner_pos, 0), (1, 1, PATCH_DEV))[0, 0] - owner_pos
    )
    stays = own_offset == 0
    paired = jnp.stack([previous, predicted], axis=1)
    to_right, to_left = pack_movers(own_offset, paired)
    arrived = []
    for shift_by, payload in ((1, to_right), (-1, to_left)):
        arrived.append(passed_along(payload, "patch", shift_by))
    kept = jnp.where(stays[:, None, None, None], paired, 0.0)
    combined = jnp.concatenate([kept, arrived[0], arrived[1]], axis=0)
    layout_ids = slot_layout(new_owner, ROWS_DEV, MOVE_CAP)
    result = newton_solve(
        combined[:, 0],
        combined[:, 1],
        layout_ids,
        band_pos,
        owner_pos,
        levels,
        diffusion,
        decay,
        reaction,
    )
    return result[None, None]


def solution(mesh):
    placed = (
        P("grp", "patch", None, None, None),
        P("grp", "patch", None, None, None),
        P(),
        P(),
        P(),
        P(),
        P(),
    )
    return jax.shard_map(
        per_device,
        mesh=mesh,
        in_specs=placed,
        out_specs=P("grp", "patch", None, None, None),
        check_vma=False,
    )
```

profile of v0, /device:TPU:0, one launch (start us, length us, event | category | flops | bytes accessed | tf_op | source)
XLA Modules:
  0.0 950.1 jit_solution(16144028055857407101)
XLA Ops:
  5.7 4.9 collective-permute-start
  29.4 4.6 copy.1013
  38.6 4.6 collective-permute-start.2
  45.2 4.7 collective-permute-done.3
  80.8 58.1 %psum.98 = f32[]{:T(128)} all-reduce(f32[]{:T(128)} %get-tuple-element.480), channel_id=1, replica_groups=mesh['patch'=8,'grp'=4] {'patch','grp'}, use_global_device_ids=true, to_apply=%region_13.15 | all-reduce | flops 1 | bytes 8 | tf_op jit(solution)/shard_map/psum | solution.py:258
  144.9 4.6 copy.1020
  197.1 46.1 %all-reduce.42 = (f32[]{:T(128)}, f32[1]{0:T(128)}) all-reduce(f32[]{:T(128)} %get-tuple-element.482, f32[1]{0:T(128)} %bitcast.89), channel_id=1, replica_groups=mesh['patch'=8,'grp'=4] {'patch','grp'}, use_global_device_ids=true, to_apply=%region_16.18 | all-reduce | flops 2 | bytes 16 | tf_op jit(solution)/shard_map/psum | solution.py:273
  250.6 4.6 copy.1027
  300.3 6.2 convolution_bitcast_fusion.9
  306.5 45.8 %all-reduce.41 = (f32[2]{0:T(128)S(1)}, f32[]{:T(128)}) all-reduce(f32[2]{0:T(128)S(1)} %convolution_bitcast_fusion.9, f32[]{:T(128)} %get-tuple-element.484), channel_id=1, replica_groups=mesh['patch'=8,'grp'=4] {'patch','grp'}, use_global_device_ids=true, to_apply=%region_18.20 | all-reduce | flops 3 | bytes 24 | tf_op jit(solution)/shard_map/psum | solution.py:273
  366.1 4.6 copy.1034
  375.3 4.2 collective-permute-start.14
  417.7 6.0 fusion.24
  423.7 44.5 %all-reduce.40 = (f32[3]{0:T(128)S(1)}, f32[]{:T(128)}) all-reduce(f32[3]{0:T(128)S(1)} %fusion.24, f32[]{:T(128)} %get-tuple-element.486), channel_id=1, replica_groups=mesh['patch'=8,'grp'=4] {'patch','grp'}, use_global_device_ids=true, to_apply=%region_23.25 | all-reduce | flops 4 | bytes 32 | tf_op jit(solution)/shard_map/psum | solution.py:273
  495.6 4.6 copy.1041
  544.2 45.9 %psum.105 = f32[]{:T(128)} all-reduce(f32[]{:T(128)} %get-tuple-element.488), channel_id=1, replica_groups=mesh['patch'=8,'grp'=4] {'patch','grp'}, use_global_device_ids=true, to_apply=%region_28.30 | all-reduce | flops 1 | bytes 8 | tf_op jit(solution)/shard_map/psum | solution.py:258
  597.8 4.6 copy.1048
  647.8 46.1 %all-reduce.39 = (f32[]{:T(128)}, f32[1]{0:T(128)}) all-reduce(f32[]{:T(128)} %get-tuple-element.490, f32[1]{0:T(128)} %bitcast.205), channel_id=1, replica_groups=mesh['patch'=8,'grp'=4] {'patch','grp'}, use_global_device_ids=true, to_apply=%region_31.33 | all-reduce | flops 2 | bytes 16 | tf_op jit(solution)/shard_map/psum | solution.py:273
  703.7 4.6 copy.1055
  753.2 6.3 convolution_bitcast_fusion.8
  759.6 45.7 %all-reduce.38 = (f32[2]{0:T(128)S(1)}, f32[]{:T(128)}) all-reduce(f32[2]{0:T(128)S(1)} %convolution_bitcast_fusion.8, f32[]{:T(128)} %get-tuple-element.492), channel_id=1, replica_groups=mesh['patch'=8,'grp'=4] {'patch','grp'}, use_global_device_ids=true, to_apply=%region_32.34 | all-reduce | flops 3 | bytes 24 | tf_op jit(solution)/shard_map/psum | solution.py:273
  826.1 4.2 collective-permute-start.30
  875.4 6.0 fusion.27
  881.4 44.9 %all-reduce.37 = (f32[3]{0:T(128)S(1)}, f32[]{:T(128)}) all-reduce(f32[3]{0:T(128)S(1)} %fusion.27, f32[]{:T(128)} %get-tuple-element.494), channel_id=1, replica_groups=mesh['patch'=8,'grp'=4] {'patch','grp'}, use_global_device_ids=true, to_apply=%region_36.38 | all-reduce | flops 4 | bytes 32 | tf_op jit(solution)/shard_map/psum | solution.py:273
  (765 shorter events, 456.8 us)
Async XLA Ops:
  5.7 15.7 %collective-permute-start = (f32[2,2,21,256]{3,2,0,1:T(8,128)S(1)}, f32[2,2,21,256]{3,2,0,1:T(8,128)S(1)}, u32[]{:S(2)}, u32[]{:S(2)}) collective-permute-start(f32[2,2,21,256]{3,2,0,1:T(8,128)S(1)} %fusion.150), channel_id=1, source_target_pairs={{0,4},{4,8},{8,12},{12,16},{16,20},{20,24},{24,28},{1,5},{5,9},{9,... | collective-permute-start | bytes 258056 | tf_op jit(solution)/shard_map/ppermute | solution.py:38
  11.8 9.7 %collective-permute-start.1 = (f32[2,2,21,256]{3,2,0,1:T(8,128)S(1)}, f32[2,2,21,256]{3,2,0,1:T(8,128)S(1)}, u32[]{:S(2)}, u32[]{:S(2)}) collective-permute-start(f32[2,2,21,256]{3,2,0,1:T(8,128)S(1)} %fusion.149), channel_id=1, source_target_pairs={{4,0},{8,4},{12,8},{16,12},{20,16},{24,20},{28,24},{5,1},{9,5},{13... | collective-permute-start | bytes 258056 | tf_op jit(solution)/shard_map/ppermute | solution.py:38
  38.6 6.6 collective-permute-start.2
  43.2 6.8 collective-permute-start.3
  51.5 5.3 collective-permute-start.5
  154.1 7.1 collective-permute-start.6
  158.2 6.4 collective-permute-start.7
  259.6 7.1 collective-permute-start.10
  263.8 6.4 collective-permute-start.11
  270.4 5.5 collective-permute-start.12
  375.3 8.5 collective-permute-start.14
  379.5 6.4 collective-permute-start.15
  386.1 6.6 collective-permute-start.16
  387.4 5.2 collective-permute-start.17
  504.5 7.1 collective-permute-start.18
  508.7 6.4 collective-permute-start.19
  606.9 7.1 collective-permute-start.22
  611.1 6.4 collective-permute-start.23
  712.9 7.1 collective-permute-start.26
  717.1 6.4 collective-permute-start.27
  723.7 5.4 collective-permute-start.28
  826.1 8.6 collective-permute-start.30
  830.3 6.4 collective-permute-start.31
  836.9 6.2 collective-permute-start.32
  (166 other events, 1072.1 us)
where the time goes:
time: 960 us; the launch traced here: 950 us
  blocking collectives  377 us (39%)
  local copies, waits for them, and re-layouts  290 us (30%)
  matrix products  97.2 us (10%)
  starting transfers between devices  72.8 us (8%)
  other arithmetic  42.3 us (4%)
  between operations  36.8 us (4%)
  waiting for transfers between devices  34.1 us (4%)
    psum x6, blocking collectives, newton_solve(): lax.psum((local_products, jnp.sum(image * image)), ('patch', 'grp'))  273 us
    psum x2, blocking collectives, newton_solve(): squares = lax.psum(jnp.sum(resid * resid), ('patch', 'grp'))  104 us
    unnamed x331, local copies, waits for them, and re-layouts  62.2 us
    ppermute x16, starting transfers between devices, extended(): before = lax.ppermute(last, axis, up)  45.1 us
    dot_general x32, matrix products, neighbor_strips(): jnp.dot(selector, candidates, precision=highest, preferred_element_type=j...  31.4 us
    another operation x16, local copies, waits for them, and re-layouts, laplace_slots(): jnp.tile(ghosts[3], (1, 1, CELLS))  30 us
    ppermute x16, waiting for transfers between devices, extended(): after = lax.ppermute(initial, axis, down)  29.7 us
    dot_general x8, matrix products, mixing(): return jnp.einsum('st,kta->ksa', reaction, values, precision=highest)  28.8 us
  transfers between devices with their start and end apart: 34, of which 18 were waited for; matrix products, arithmetic and copies ran while one was open for 4% of the time, Pallas kernels for 0%

commit v1 on v0

v1 whole, which is shorter than its diff:
```python
import functools

import jax
import jax.numpy as jnp
from jax import lax
from jax.experimental import pallas as pl
from jax.experimental.pallas import tpu as pltpu
from jax.sharding import PartitionSpec as P

CELLS = 16
ROWS = 4
MOVE_CAP = 2
KRYLOV = 3
NEWTON = 2

step_rate = 4.0
epsilon = 1e-12
highest = lax.Precision.HIGHEST
SHIFT = 16.0
SCALE = 64.0
PAIRS = [(i, j) for j in range(KRYLOV + 1) for i in range(j + 1)]
DIRECTIONS = [(x, y) for x in (-1, 0, 1) for y in (-1, 0, 1) if (x, y) != (0, 0)]


def small_solve(matrix, vector):
    dimension = len(vector)
    matrix = [list(line) for line in matrix]
    vector = list(vector)
    for column_at in range(dimension):
        for target in range(column_at + 1, dimension):
            factor = matrix[target][column_at] / matrix[column_at][column_at]
            for k in range(column_at, dimension):
                matrix[target][k] = matrix[target][k] - factor * matrix[column_at][k]
            vector[target] = vector[target] - factor * vector[column_at]
    answer = [None] * dimension
    for column_at in reversed(range(dimension)):
        running = vector[column_at]
        for later in range(column_at + 1, dimension):
            running = running - matrix[column_at][later] * answer[later]
        answer[column_at] = running / matrix[column_at][column_at]
    return answer


def add(a, b):
    return b if a is None else a if b is None else a + b


def total(terms):
    result = None
    for term in terms:
        result = add(result, term)
    return result


def krylov_weights(gram):
    size = KRYLOV + 1

    def inner(a, b):
        return total(
            a[i] * b[j] * gram[min(i, j), max(i, j)]
            for i in range(size)
            for j in range(size)
            if a[i] is not None and b[j] is not None
        )

    beta = jnp.sqrt(gram[0, 0] + epsilon)
    basis = [[-1.0 / beta] + [None] * KRYLOV]
    hess = [[None] * KRYLOV for _ in range(size)]
    for j in range(KRYLOV):
        current = basis[j]
        image = [None] * size
        for i in range(size):
            if current[i] is not None:
                image[i] = add(image[i], SHIFT * current[i])
                image[i + 1] = add(image[i + 1], SCALE * current[i])
        coeffs = [inner(image, vector) for vector in basis]
        for i, vector in enumerate(basis):
            hess[i][j] = coeffs[i]
            image = [
                a if b is None else a - coeffs[i] * b for a, b in zip(image, vector)
            ]
        height = jnp.sqrt(jnp.maximum(inner(image, image), 0.0) + epsilon)
        hess[j + 1][j] = height
        basis.append([None if a is None else a / height for a in image])
    normal = [
        [
            total(
                hess[k][a] * hess[k][b]
                for k in range(size)
                if hess[k][a] is not None and hess[k][b] is not None
            )
            for b in range(KRYLOV)
        ]
        for a in range(KRYLOV)
    ]
    y = small_solve(normal, [beta * hess[0][b] for b in range(KRYLOV)])
    return [
        total(y[j] * basis[j][i] for j in range(KRYLOV) if basis[j][i] is not None)
        for i in range(KRYLOV)
    ]


def kernel(
    owners, bands, owner_s, level_s, diff_in, decay_in, react_in, prev_in, pred_in, out,
    state, before, k0, k1, k2, k3, face, gram_a, gram_b, movers,
    local_sem, halo_send, halo_recv, a_send, a_recv, b_send, b_recv, move_send, move_recv,
):
    rows, cols, species, surface = prev_in.shape
    ext_rows, ext_cols = rows + 2, cols + 2
    me = lax.axis_index("patch")
    band = lax.axis_index("grp")
    MESH = pl.DeviceIdType.MESH

    def exists(dx, dy):
        tests = []
        if dx:
            tests.append(me < owners - 1 if dx > 0 else me > 0)
        if dy:
            tests.append(band < bands - 1 if dy > 0 else band > 0)
        return functools.reduce(jnp.logical_and, tests)

    barrier = pltpu.get_barrier_semaphore()
    for d in range(1, bands):
        pl.semaphore_signal(
            barrier, inc=1, device_id={"grp": lax.rem(band + d, bands)}, device_id_type=MESH
        )

    @pl.loop(1, owners)
    def _(d):
        pl.semaphore_signal(
            barrier, inc=1, device_id={"patch": lax.rem(me + d, owners)}, device_id_type=MESH
        )

    for dx, dy in DIRECTIONS:
        if dx and dy:
            @pl.when(exists(dx, dy))
            def _():
                pl.semaphore_signal(
                    barrier, inc=1, device_id={"patch": me + dx, "grp": band + dy},
                    device_id_type=MESH,
                )

    fields = ((pred_in, state), (prev_in, before))
    own = [
        pltpu.make_async_copy(
            src, dst.at[pl.ds(1, rows), pl.ds(1, cols)], local_sem.at[f]
        )
        for f, (src, dst) in enumerate(fields)
    ]
    for copy in own:
        copy.start()

    def span(delta, length):
        if delta == 0:
            return pl.ds(0, length), pl.ds(1, length)
        if delta > 0:
            return pl.ds(length - 1, 1), pl.ds(0, 1)
        return pl.ds(0, 1), pl.ds(length + 1, 1)

    def halo(f, at):
        dx, dy = DIRECTIONS[at]
        src, dst = fields[f]
        col_from, col_to = span(dx, cols)
        row_from, row_to = span(dy, rows)
        return pltpu.make_async_remote_copy(
            src_ref=src.at[row_from, col_from],
            dst_ref=dst.at[row_to, col_to],
            send_sem=halo_send.at[f, at],
            recv_sem=halo_recv.at[f, at],
            device_id={"patch": me + dx, "grp": band + dy},
            device_id_type=MESH,
        )

    def one(dx, dy):
        return jnp.where(exists(dx, dy), 1, 0)

    corners = (one(1, 0) + one(-1, 0)) * (one(0, 1) + one(0, -1))
    pl.semaphore_wait(barrier, bands - 1 + owners - 1 + corners)
    for at, (dx, dy) in enumerate(DIRECTIONS):
        @pl.when(exists(dx, dy))
        def _():
            for f in range(2):
                halo(f, at).start()

        @pl.when(jnp.logical_not(exists(-dx, -dy)))
        def _():
            row_to, col_to = span(dy, rows)[1], span(dx, cols)[1]
            shape = (row_to.size, col_to.size, species, surface)
            for f in range(2):
                fields[f][1][row_to, col_to] = jnp.zeros(shape, jnp.float32)

    lane = lax.broadcasted_iota(jnp.int32, (1, surface), 1)
    cell_col, cell_row = lane % CELLS, lane // CELLS
    west_edge, east_edge = cell_col == 0, cell_col == CELLS - 1
    south_edge, north_edge = cell_row == 0, cell_row == CELLS - 1
    diagonal = lax.broadcasted_iota(jnp.int32, (species, species), 0) == (
        lax.broadcasted_iota(jnp.int32, (species, species), 1)
    )

    def column(ref):
        return jnp.sum(jnp.where(diagonal, ref[...], 0.0), axis=1, keepdims=True)

    diffusion, decay = column(diff_in), column(decay_in)
    kind = lax.broadcasted_iota(jnp.int32, (species, 1), 0)
    rate = jnp.where(kind < species - 1, step_rate, 0.0)
    reaction = react_in[...]
    reaction_a = reaction * (1.0 / SCALE)
    diffusion_a = diffusion * (1.0 / SCALE)
    decay_a = decay * (3.0 / SCALE)
    rate_a = (rate - SHIFT) * (1.0 / SCALE)

    def kappa(r, c):
        row = jnp.clip(band * rows + r - 1, 0, bands * rows - 1)
        col = jnp.clip(me * cols + c - 1, 0, owners * cols - 1)
        level = level_s[row // rows, col // cols, (row % rows) * cols + col % cols]
        return jnp.where(level == 0, 1.0, jnp.where(level == 1, 4.0, 16.0))

    @pl.loop(0, ext_rows)
    def _(r):
        for c in range(ext_cols):
            mid = kappa(r, c)
            west = jnp.where(west_edge, 0.5 * (mid + kappa(r, c - 1)), mid)
            east = jnp.where(east_edge, 0.5 * (mid + kappa(r, c + 1)), mid)
            south = jnp.where(south_edge, 0.5 * (mid + kappa(r - 1, c)), mid)
            north = jnp.where(north_edge, 0.5 * (mid + kappa(r + 1, c)), mid)
            for d, value in enumerate((west, east, south, north)):
                face[r, c, pl.ds(d, 1), :] = value
            face[r, c, pl.ds(4, 1), :] = west + east + south + north

    for copy in own:
        copy.wait()
    for at, (dx, dy) in enumerate(DIRECTIONS):
        @pl.when(exists(-dx, -dy))
        def _():
            for f in range(2):
                halo(f, at).wait_recv()

    def inside(r, c):
        row, col = band * rows + r - 1, me * cols + c - 1
        good = (row >= 0) & (row < bands * rows) & (col >= 0) & (col < owners * cols)
        return jnp.where(good, 1.0, 0.0)

    def sweep(src, dst, finish, mix, row_from, row_to, col_from, col_to):
        @pl.loop(row_from, row_to)
        def _(r):
            below, above = jnp.maximum(r - 1, 0), jnp.minimum(r + 1, ext_rows - 1)
            for c in range(col_from, col_to):
                x = src[r, c]
                west = jnp.where(
                    west_edge,
                    pltpu.roll(src[r, max(c - 1, 0)], surface - CELLS + 1, 1),
                    pltpu.roll(x, 1, 1),
                )
                east = jnp.where(
                    east_edge,
                    pltpu.roll(src[r, min(c + 1, ext_cols - 1)], CELLS - 1, 1),
                    pltpu.roll(x, surface - 1, 1),
                )
                south = pltpu.roll(jnp.where(north_edge, src[below, c], x), CELLS, 1)
                north = pltpu.roll(jnp.where(south_edge, src[above, c], x), surface - CELLS, 1)
                lap = (
                    face[r, c, pl.ds(0, 1), :] * west
                    + face[r, c, pl.ds(1, 1), :] * east
                    + face[r, c, pl.ds(2, 1), :] * south
                    + face[r, c, pl.ds(3, 1), :] * north
                    - face[r, c, pl.ds(4, 1), :] * x
                )
                mixed = jnp.dot(mix, x, precision=highest, preferred_element_type=jnp.float32)
                dst[r, c] = finish(r, c, x, lap, mixed) * inside(r, c)

    def residual(r, c, x, lap, mixed):
        return rate * (x - before[r, c]) - diffusion * lap - mixed + decay * (x * x * x)

    def jacobian(r, c, x, lap, mixed):
        u = state[r, c]
        return (rate_a + decay_a * (u * u)) * x - diffusion_a * lap - mixed

    krylov = (k0, k1, k2, k3)
    everywhere = (0, ext_rows, 0, ext_cols)
    own_only = (1, rows + 1, 1, cols + 1)
    out_lane = lax.broadcasted_iota(jnp.int32, (1, 128), 1)

    for newton_step in range(NEWTON):
        sweep(state, k0, residual, reaction, *everywhere)
        for j in range(KRYLOV):
            sweep(
                krylov[j], krylov[j + 1], jacobian, reaction_a,
                *(everywhere if j < KRYLOV - 1 else own_only),
            )
        line = jnp.zeros((1, 128), jnp.float32)
        for at, (i, j) in enumerate(PAIRS):
            def products(r, acc, i=i, j=j):
                for c in range(1, cols + 1):
                    acc = acc + krylov[i][r, c] * krylov[j][r, c]
                return acc

            acc = lax.fori_loop(
                1, rows + 1, products, jnp.zeros((species, surface), jnp.float32)
            )
            value = jnp.sum(jnp.sum(acc, axis=0, keepdims=True), axis=1, keepdims=True)
            line = line + jnp.where(out_lane == at, value, 0.0)

        gram_a[newton_step, band] = line

        def send_a(d, slot, target):
            return pltpu.make_async_remote_copy(
                src_ref=gram_a.at[newton_step, slot],
                dst_ref=gram_a.at[newton_step, slot],
                send_sem=a_send.at[newton_step, d],
                recv_sem=a_recv.at[newton_step, d],
                device_id={"grp": target},
                device_id_type=MESH,
            )

        def send_b(d, slot, target):
            return pltpu.make_async_remote_copy(
                src_ref=gram_b.at[newton_step, slot],
                dst_ref=gram_b.at[newton_step, slot],
                send_sem=b_send.at[newton_step, d],
                recv_sem=b_recv.at[newton_step, d],
                device_id={"patch": target},
                device_id_type=MESH,
            )

        for d in range(1, bands):
            send_a(d, band, lax.rem(band + d, bands)).start()
        for d in range(1, bands):
            send_a(d, lax.rem(band + bands - d, bands), band).wait_recv()
        part = gram_a[newton_step, 0]
        for d in range(1, bands):
            part = part + gram_a[newton_step, d]
        gram_b[newton_step, me] = part

        @pl.loop(1, owners)
        def _(d):
            send_b(d, me, lax.rem(me + d, owners)).start()

        @pl.loop(1, owners)
        def _(d):
            send_b(d, lax.rem(me + owners - d, owners), me).wait_recv()

        whole = gram_b[newton_step, 0]
        for d in range(1, owners):
            whole = whole + gram_b[newton_step, d]
        gram = {
            pair: jnp.sum(jnp.where(out_lane == at, whole, 0.0), axis=1, keepdims=True)
            for at, pair in enumerate(PAIRS)
        }
        weights = [
            jnp.broadcast_to(w, (1, surface)) for w in krylov_weights(gram)
        ]

        row_from, row_to, col_from, col_to = (
            everywhere if newton_step < NEWTON - 1 else own_only
        )

        @pl.loop(row_from, row_to)
        def _(r):
            for c in range(col_from, col_to):
                state[r, c] = state[r, c] + (
                    weights[0] * k0[r, c] + weights[1] * k1[r, c] + weights[2] * k2[r, c]
                )

        for d in range(1, bands):
            send_a(d, band, band).wait_send()

        @pl.loop(1, owners)
        def _(d):
            send_b(d, me, me).wait_send()

    def new_owner(r, c):
        return owner_s[band, me, (r - 1) * cols + c - 1]

    slots = rows * cols
    for side, (c, step) in enumerate(((cols, 1), (1, -1))):
        rank = jnp.int32(0)
        packed = [jnp.zeros((species, surface), jnp.float32) for _ in range(MOVE_CAP)]
        for r in range(1, rows + 1):
            moving = new_owner(r, c) == me + step
            for m in range(MOVE_CAP):
                packed[m] = jnp.where(moving & (rank == m), state[r, c], packed[m])
            rank = rank + jnp.where(moving, 1, 0)
        for m in range(MOVE_CAP):
            movers[side, m] = packed[m]

    def move(side, step):
        return pltpu.make_async_remote_copy(
            src_ref=movers.at[side],
            dst_ref=out.at[pl.ds(slots + side * MOVE_CAP, MOVE_CAP)],
            send_sem=move_send.at[side],
            recv_sem=move_recv.at[side],
            device_id={"patch": me + step},
            device_id_type=MESH,
        )

    for side, step in enumerate((1, -1)):
        @pl.when(exists(step, 0))
        def _():
            move(side, step).start()

        @pl.when(jnp.logical_not(exists(-step, 0)))
        def _():
            out[pl.ds(slots + side * MOVE_CAP, MOVE_CAP)] = jnp.zeros(
                (MOVE_CAP, species, surface), jnp.float32
            )

    for r in range(1, rows + 1):
        for c in range(1, cols + 1):
            stays = new_owner(r, c) == me
            out[(r - 1) * cols + c - 1] = jnp.where(stays, state[r, c], 0.0)

    for at, (dx, dy) in enumerate(DIRECTIONS):
        @pl.when(exists(dx, dy))
        def _():
            for f in range(2):
                halo(f, at).wait_send()

    for side, step in enumerate((1, -1)):
        @pl.when(exists(-step, 0))
        def _():
            move(side, step).wait_recv()

        @pl.when(exists(step, 0))
        def _():
            move(side, step).wait_send()


def per_device(owners, bands, previous, predicted, new_owner, levels, diffusion, decay, reaction):
    patches, species, surface = previous.shape[2:]
    cols = patches // ROWS
    ext = (ROWS + 2, cols + 2, species, surface)
    grid = (ROWS, cols, species, surface)
    vmem = pl.BlockSpec(memory_space=pltpu.VMEM)
    smem = pl.BlockSpec(memory_space=pltpu.SMEM)
    anywhere = pl.BlockSpec(memory_space=pl.ANY)
    dma = pltpu.SemaphoreType.DMA
    result = pl.pallas_call(
        functools.partial(kernel, owners, bands),
        out_shape=jax.ShapeDtypeStruct((patches + 2 * MOVE_CAP, species, surface), jnp.float32),
        in_specs=[smem, smem, vmem, vmem, vmem, anywhere, anywhere],
        out_specs=vmem,
        scratch_shapes=[
            *[pltpu.VMEM(ext, jnp.float32) for _ in range(KRYLOV + 3)],
            pltpu.VMEM((ROWS + 2, cols + 2, 8, surface), jnp.float32),
            pltpu.VMEM((NEWTON, bands, 1, 128), jnp.float32),
            pltpu.VMEM((NEWTON, owners, 1, 128), jnp.float32),
            pltpu.VMEM((2, MOVE_CAP, species, surface), jnp.float32),
            dma((2,)),
            dma((2, len(DIRECTIONS))),
            dma((2, len(DIRECTIONS))),
            dma((NEWTON, bands)),
            dma((NEWTON, bands)),
            dma((NEWTON, owners)),
            dma((NEWTON, owners)),
            dma((2,)),
            dma((2,)),
        ],
        compiler_params=pltpu.CompilerParams(collective_id=0, has_side_effects=True),
    )(
        new_owner,
        levels,
        diffusion.reshape(1, species),
        decay.reshape(1, species),
        reaction,
        previous.reshape(grid),
        predicted.reshape(grid),
    )
    return result[None, None]


def solution(mesh):
    placed = (P("grp", "patch"), P("grp", "patch"), P(), P(), P(), P(), P())
    return jax.shard_map(
        functools.partial(per_device, mesh.shape["patch"], mesh.shape["grp"]),
        mesh=mesh,
        in_specs=placed,
        out_specs=P("grp", "patch"),
        check_vma=False,
    )
```

time: 960 us -> 57.5 us (0.06)
  blocking collectives: 377 us -> 0 us
  local copies, waits for them, and re-layouts: 290 us -> 4.31 us
  matrix products: 97.2 us -> 0 us
  starting transfers between devices: 72.8 us -> 0 us
  Pallas kernels: 0 us -> 52.9 us
  other arithmetic: 42.3 us -> 0 us
  between operations: 36.8 us -> 0.01 us
  waiting for transfers between devices: 34.1 us -> 0 us
    psum x8 -> x0, blocking collectives: 377 us -> none  [the longest x6 273 us: newton_solve(): lax.psum((local_products, jnp.sum(image * image)), ('patch', 'grp'))]
    dot_general x50 -> x0, matrix products: 97.2 us -> none  [the longest x32 31.4 us: neighbor_strips(): jnp.dot(selector, candidates, precision=highest, preferred_element_type=j...]
    ppermute x34 -> x0, starting transfers between devices: 72.8 us -> none  [the longest x16 45.1 us: extended(): before = lax.ppermute(last, axis, up)]
    slice x49 -> x0, local copies, waits for them, and re-layouts: 62.9 us -> none  [the longest x8 26.7 us: neighbor_strips(): squared[:, :, :, 0]]
    unnamed x331 -> x4, local copies, waits for them, and re-layouts: 62.2 us -> 2.47 us
    another operation x49 -> x0, local copies, waits for them, and re-layouts: 56.5 us -> none  [the longest x16 30 us: laplace_slots(): jnp.tile(ghosts[3], (1, 1, CELLS))]
    pallas_call x0 -> x1, Pallas kernels: none -> 52.9 us  [per_device(): pl.pallas_call(functools.partial(kernel, owners, bands), out_shape=jax.Sh...]
    reshape x40 -> x0, local copies, waits for them, and re-layouts: 50.7 us -> none  [the longest x8 15.9 us: laplace_slots(): jnp.repeat(ghosts[1], CELLS, axis=-1)]
  transfers between devices with their start and end apart: 34 -> 0, of which waited for: 18 -> 0; matrix products, arithmetic and copies ran while one was open for 4% -> 0% of each run, Pallas kernels for 0% -> 0%
where the time goes in v1:
time: 57.5 us; the launch traced here: 57.2 us
  Pallas kernels  52.9 us (92%)
  local copies, waits for them, and re-layouts  4.31 us (7%)
    pallas_call x1, Pallas kernels, per_device(): pl.pallas_call(functools.partial(kernel, owners, bands), out_shape=jax.Sh...  52.9 us
    unnamed x4, local copies, waits for them, and re-layouts  2.47 us
    broadcast_in_dim x1, local copies, waits for them, and re-layouts, per_device(): return result[None, None]  1.84 us

profile of v1, /device:TPU:0, one launch (start us, length us, event | category | flops | bytes accessed | tf_op | source)
XLA Modules:
  0.0 57.2 jit_solution(12709840839919277181)
XLA Ops:
  0.0 0.0 copy-start
  0.0 1.7 %copy.10 = f32[1,1,12,21,256]{4,3,1,2,0:T(8,128)} copy(f32[1,1,12,21,256]{4,1,3,2,0:T(1,128)} %param.7) | data formatting | bytes 516096
  1.7 0.0 copy-done
  1.7 0.7 %copy.11 = f32[1,1,12,21,256]{4,3,1,2,0:T(8,128)} copy(f32[1,1,12,21,256]{4,1,3,2,0:T(1,128)S(1)} %copy-done) | data formatting | bytes 516096
  2.5 52.9 %shard_map.73 = f32[16,21,256]{2,1,0:T(8,128)} custom-call(s32[4,8,12]{2,1,0:T(8,128)} %owner_s.1, s32[4,8,12]{2,1,0:T(8,128)} %level_s.1, f32[1,21]{1,0:T(1,128)} %bitcast.8, f32[1,21]{1,0:T(1,128)} %bitcast.9, f32[21,21]{1,0:T(8,128)} %react_in.1, f32[4,3,21,256]{3,2,1,0:T(8,128)} %bitcast.6, f32[4,3,21,256]{3,2,1,0:T(8,128)} %bitcast.7), custom_call_target="tpu_custom_call" | custom-call | tf_op jit(solution)/shard_map/pallas_call | solution.py:437
  55.4 1.8 %copy.9 = f32[1,1,16,21,256]{4,2,3,1,0:T(8,128)} copy(f32[1,1,16,21,256]{4,3,2,1,0:T(8,128)} %bitcast.5) | data formatting | bytes 688128 | tf_op jit(solution)/shard_map/broadcast_in_dim | solution.py:468
Async XLA Ops:
  0.0 1.7 %copy-start = (f32[1,1,12,21,256]{4,1,3,2,0:T(1,128)S(1)}, f32[1,1,12,21,256]{4,1,3,2,0:T(1,128)}, u32[]{:S(2)}) copy-start(f32[1,1,12,21,256]{4,1,3,2,0:T(1,128)} %param.8) | copy-start | bytes 774148

commit v2 on v1

--- a/solution.py
+++ b/solution.py
@@ -102,7 +102,7 @@
 
 def kernel(
     owners, bands, owner_s, level_s, diff_in, decay_in, react_in, prev_in, pred_in, out,
-    state, before, k0, k1, k2, k3, face, gram_a, gram_b, movers,
+    state, before, k0, k1, k2, k3, face, gram_a, gram_b, movers, landing, strip_out, strip_in,
     local_sem, halo_send, halo_recv, a_send, a_recv, b_send, b_recv, move_send, move_recv,
 ):
     rows, cols, species, surface = prev_in.shape
@@ -150,6 +150,10 @@
     for copy in own:
         copy.start()
 
+    half = surface // 2
+    low, high = pl.ds(0, half), pl.ds(half, half)
+    pairs = rows // 2
+
     def span(delta, length):
         if delta == 0:
             return pl.ds(0, length), pl.ds(1, length)
@@ -160,17 +164,42 @@
     def halo(f, at):
         dx, dy = DIRECTIONS[at]
         src, dst = fields[f]
-        col_from, col_to = span(dx, cols)
-        row_from, row_to = span(dy, rows)
+        if dy == 0:
+            side = 0 if dx > 0 else 1
+            source, target = strip_out.at[f, side], strip_in.at[f, side]
+        else:
+            lanes = high if dy > 0 else low
+            col_from, col_to = span(dx, cols)
+            row_from, row_to = span(dy, rows)
+            source = src.at[row_from, col_from, :, lanes]
+            target = dst.at[row_to, col_to, :, lanes]
         return pltpu.make_async_remote_copy(
-            src_ref=src.at[row_from, col_from],
-            dst_ref=dst.at[row_to, col_to],
+            src_ref=source,
+            dst_ref=target,
             send_sem=halo_send.at[f, at],
             recv_sem=halo_recv.at[f, at],
             device_id={"patch": me + dx, "grp": band + dy},
             device_id_type=MESH,
         )
 
+    lane = lax.broadcasted_iota(jnp.int32, (1, surface), 1)
+    cell_col, cell_row = lane % CELLS, lane // CELLS
+    right_half = cell_col >= CELLS // 2
+
+    for copy in own:
+        copy.wait()
+    for f in range(2):
+        field = fields[f][1]
+        for k in range(pairs):
+            first, second = field[2 * k + 1, cols], field[2 * k + 2, cols]
+            strip_out[f, 0, k] = jnp.where(
+                right_half, first, pltpu.roll(second, surface - CELLS // 2, 1)
+            )
+            first, second = field[2 * k + 1, 1], field[2 * k + 2, 1]
+            strip_out[f, 1, k] = jnp.where(
+                right_half, pltpu.roll(second, CELLS // 2, 1), first
+            )
+
     def one(dx, dy):
         return jnp.where(exists(dx, dy), 1, 0)
 
@@ -185,12 +214,11 @@
         @pl.when(jnp.logical_not(exists(-dx, -dy)))
         def _():
             row_to, col_to = span(dy, rows)[1], span(dx, cols)[1]
-            shape = (row_to.size, col_to.size, species, surface)
+            lanes = pl.ds(0, surface) if dy == 0 else high if dy > 0 else low
+            shape = (row_to.size, col_to.size, species, lanes.size)
             for f in range(2):
-                fields[f][1][row_to, col_to] = jnp.zeros(shape, jnp.float32)
-
-    lane = lax.broadcasted_iota(jnp.int32, (1, surface), 1)
-    cell_col, cell_row = lane % CELLS, lane // CELLS
+                fields[f][1][row_to, col_to, :, lanes] = jnp.zeros(shape, jnp.float32)
+
     west_edge, east_edge = cell_col == 0, cell_col == CELLS - 1
     south_edge, north_edge = cell_row == 0, cell_row == CELLS - 1
     diagonal = lax.broadcasted_iota(jnp.int32, (species, species), 0) == (
@@ -227,66 +255,151 @@
                 face[r, c, pl.ds(d, 1), :] = value
             face[r, c, pl.ds(4, 1), :] = west + east + south + north
 
-    for copy in own:
-        copy.wait()
     for at, (dx, dy) in enumerate(DIRECTIONS):
         @pl.when(exists(-dx, -dy))
         def _():
             for f in range(2):
                 halo(f, at).wait_recv()
+            if dy == 0:
+                for f in range(2):
+                    for k in range(pairs):
+                        strip = strip_in[f, 0 if dx > 0 else 1, k]
+                        at_col = 0 if dx > 0 else cols + 1
+                        shift = CELLS // 2 if dx > 0 else surface - CELLS // 2
+                        fields[f][1][2 * k + 1, at_col] = strip
+                        fields[f][1][2 * k + 2, at_col] = pltpu.roll(strip, shift, 1)
 
     def inside(r, c):
         row, col = band * rows + r - 1, me * cols + c - 1
         good = (row >= 0) & (row < bands * rows) & (col >= 0) & (col < owners * cols)
         return jnp.where(good, 1.0, 0.0)
 
-    def sweep(src, dst, finish, mix, row_from, row_to, col_from, col_to):
-        @pl.loop(row_from, row_to)
+    def edges(width):
+        column = lax.broadcasted_iota(jnp.int32, (1, width), 1)
+        return (
+            column % CELLS == 0,
+            column % CELLS == CELLS - 1,
+            column < CELLS,
+            column >= width - CELLS,
+        )
+
+    whole_edges, half_edges = edges(surface), edges(half)
+
+    def patch(src, dst, finish, r, c, lanes, below, above):
+        width = lanes.size
+        at_west, at_east, at_south, at_north = (
+            whole_edges if width == surface else half_edges
+        )
+        x = src[r, c, :, lanes]
+        left = src[r, max(c - 1, 0), :, lanes]
+        right = src[r, min(c + 1, ext_cols - 1), :, lanes]
+        under = x if below is None else src[below[0], c, :, below[1]]
+        over = x if above is None else src[above[0], c, :, above[1]]
+        west = jnp.where(
+            at_west, pltpu.roll(left, width - CELLS + 1, 1), pltpu.roll(x, 1, 1)
+        )
+        east = jnp.where(
+            at_east, pltpu.roll(right, CELLS - 1, 1), pltpu.roll(x, width - 1, 1)
+        )
+        south = pltpu.roll(jnp.where(at_north, under, x), CELLS, 1)
+        north = pltpu.roll(jnp.where(at_south, over, x), width - CELLS, 1)
+        lap = (
+            face[r, c, pl.ds(0, 1), lanes] * west
+            + face[r, c, pl.ds(1, 1), lanes] * east
+            + face[r, c, pl.ds(2, 1), lanes] * south
+            + face[r, c, pl.ds(3, 1), lanes] * north
+            - face[r, c, pl.ds(4, 1), lanes] * x
+        )
+        dst[r, c, :, lanes] = finish(r, c, lanes, x, lap)
+
+    full = pl.ds(0, surface)
+
+    def sweep(src, dst, finish, ring):
+        col_from, col_to = (0, ext_cols) if ring else (1, cols + 1)
+
+        def masked(r, c, lanes, x, lap):
+            return finish(r, c, lanes, x, lap) * inside(r, c)
+
+        last = ext_rows - 1
+        if ring:
+            for c in range(ext_cols):
+                patch(src, dst, masked, 0, c, high, None, (1, low))
+                patch(src, dst, masked, last, c, low, (last - 1, high), None)
+
+        @pl.loop(1, rows + 1)
         def _(r):
-            below, above = jnp.maximum(r - 1, 0), jnp.minimum(r + 1, ext_rows - 1)
             for c in range(col_from, col_to):
-                x = src[r, c]
-                west = jnp.where(
-                    west_edge,
-                    pltpu.roll(src[r, max(c - 1, 0)], surface - CELLS + 1, 1),
-                    pltpu.roll(x, 1, 1),
+                patch(
+                    src, dst, masked if c in (0, cols + 1) else finish,
+                    r, c, full, (r - 1, full), (r + 1, full),
                 )
-                east = jnp.where(
-                    east_edge,
-                    pltpu.roll(src[r, min(c + 1, ext_cols - 1)], CELLS - 1, 1),
-                    pltpu.roll(x, surface - 1, 1),
-                )
-                south = pltpu.roll(jnp.where(north_edge, src[below, c], x), CELLS, 1)
-                north = pltpu.roll(jnp.where(south_edge, src[above, c], x), surface - CELLS, 1)
-                lap = (
-                    face[r, c, pl.ds(0, 1), :] * west
-                    + face[r, c, pl.ds(1, 1), :] * east
-                    + face[r, c, pl.ds(2, 1), :] * south
-                    + face[r, c, pl.ds(3, 1), :] * north
-                    - face[r, c, pl.ds(4, 1), :] * x
-                )
-                mixed = jnp.dot(mix, x, precision=highest, preferred_element_type=jnp.float32)
-                dst[r, c] = finish(r, c, x, lap, mixed) * inside(r, c)
-
-    def residual(r, c, x, lap, mixed):
-        return rate * (x - before[r, c]) - diffusion * lap - mixed + decay * (x * x * x)
-
-    def jacobian(r, c, x, lap, mixed):
-        u = state[r, c]
-        return (rate_a + decay_a * (u * u)) * x - diffusion_a * lap - mixed
+
+    def split(value):
+        big = value.astype(jnp.bfloat16)
+        return big, (value - big.astype(jnp.float32)).astype(jnp.bfloat16)
+
+    react_big, react_small = split(reaction_a)
+
+    def mixing(x):
+        big, small = split(x)
+
+        def product(a, b):
+            return jnp.dot(a, b, preferred_element_type=jnp.float32)
+
+        return product(react_small, big) + product(react_big, small) + product(react_big, big)
+
+    def residual(r, c, lanes, x, lap):
+        mixed = jnp.dot(reaction, x, precision=highest, preferred_element_type=jnp.float32)
+        old = before[r, c, :, lanes]
+        return rate * (x - old) - diffusion * lap - mixed + decay * (x * x * x)
+
+    def jacobian(r, c, lanes, x, lap):
+        u = state[r, c, :, lanes]
+        return (rate_a + decay_a * (u * u)) * x - diffusion_a * lap - mixing(x)
 
     krylov = (k0, k1, k2, k3)
-    everywhere = (0, ext_rows, 0, ext_cols)
-    own_only = (1, rows + 1, 1, cols + 1)
     out_lane = lax.broadcasted_iota(jnp.int32, (1, 128), 1)
 
+    def new_owner(r, c):
+        return owner_s[band, me, (r - 1) * cols + c - 1]
+
+    slots = rows * cols
+
+    def move(part, side, step):
+        return pltpu.make_async_remote_copy(
+            src_ref=movers.at[part, side],
+            dst_ref=landing.at[part, side],
+            send_sem=move_send.at[part, side],
+            recv_sem=move_recv.at[part, side],
+            device_id={"patch": me + step},
+            device_id_type=MESH,
+        )
+
+    def send_movers(part, field):
+        for side, (c, step) in enumerate(((cols, 1), (1, -1))):
+            rank = jnp.int32(0)
+            packed = [jnp.zeros((species, surface), jnp.float32) for _ in range(MOVE_CAP)]
+            for r in range(1, rows + 1):
+                moving = new_owner(r, c) == me + step
+                for m in range(MOVE_CAP):
+                    packed[m] = jnp.where(moving & (rank == m), field[r, c], packed[m])
+                rank = rank + jnp.where(moving, 1, 0)
+            for m in range(MOVE_CAP):
+                movers[part, side, m] = packed[m]
+        for side, step in enumerate((1, -1)):
+            @pl.when(exists(step, 0))
+            def _():
+                move(part, side, step).start()
+
     for newton_step in range(NEWTON):
-        sweep(state, k0, residual, reaction, *everywhere)
+        final = newton_step == NEWTON - 1
+        if final:
+            send_movers(0, state)
+        sweep(state, k0, residual, True)
         for j in range(KRYLOV):
-            sweep(
-                krylov[j], krylov[j + 1], jacobian, reaction_a,
-                *(everywhere if j < KRYLOV - 1 else own_only),
-            )
+            if final:
+                send_movers(j + 1, krylov[j])
+            sweep(krylov[j], krylov[j + 1], jacobian, j < KRYLOV - 1)
         line = jnp.zeros((1, 128), jnp.float32)
         for at, (i, j) in enumerate(PAIRS):
             def products(r, acc, i=i, j=j):
@@ -350,16 +463,28 @@
             jnp.broadcast_to(w, (1, surface)) for w in krylov_weights(gram)
         ]
 
-        row_from, row_to, col_from, col_to = (
-            everywhere if newton_step < NEWTON - 1 else own_only
-        )
-
-        @pl.loop(row_from, row_to)
-        def _(r):
-            for c in range(col_from, col_to):
-                state[r, c] = state[r, c] + (
-                    weights[0] * k0[r, c] + weights[1] * k1[r, c] + weights[2] * k2[r, c]
-                )
+        def update(r, c, lanes):
+            return state[r, c, :, lanes] + (
+                weights[0][:, : lanes.size] * k0[r, c, :, lanes]
+                + weights[1][:, : lanes.size] * k1[r, c, :, lanes]
+                + weights[2][:, : lanes.size] * k2[r, c, :, lanes]
+            )
+
+        if not final:
+            for c in range(ext_cols):
+                state[0, c, :, high] = update(0, c, high)
+                state[ext_rows - 1, c, :, low] = update(ext_rows - 1, c, low)
+
+            @pl.loop(1, rows + 1)
+            def _(r):
+                for c in range(ext_cols):
+                    state[r, c] = update(r, c, full)
+        else:
+            @pl.loop(1, rows + 1)
+            def _(r):
+                for c in range(1, cols + 1):
+                    stays = new_owner(r, c) == me
+                    out[(r - 1) * cols + c - 1] = jnp.where(stays, update(r, c, full), 0.0)
 
         for d in range(1, bands):
             send_a(d, band, band).wait_send()
@@ -368,61 +493,34 @@
         def _(d):
             send_b(d, me, me).wait_send()
 
-    def new_owner(r, c):
-        return owner_s[band, me, (r - 1) * cols + c - 1]
-
-    slots = rows * cols
-    for side, (c, step) in enumerate(((cols, 1), (1, -1))):
-        rank = jnp.int32(0)
-        packed = [jnp.zeros((species, surface), jnp.float32) for _ in range(MOVE_CAP)]
-        for r in range(1, rows + 1):
-            moving = new_owner(r, c) == me + step
+    for side, step in enumerate((1, -1)):
+        place = slots + side * MOVE_CAP
+
+        @pl.when(exists(-step, 0))
+        def _():
+            for part in range(KRYLOV + 1):
+                move(part, side, step).wait_recv()
             for m in range(MOVE_CAP):
-                packed[m] = jnp.where(moving & (rank == m), state[r, c], packed[m])
-            rank = rank + jnp.where(moving, 1, 0)
-        for m in range(MOVE_CAP):
-            movers[side, m] = packed[m]
-
-    def move(side, step):
-        return pltpu.make_async_remote_copy(
-            src_ref=movers.at[side],
-            dst_ref=out.at[pl.ds(slots + side * MOVE_CAP, MOVE_CAP)],
-            send_sem=move_send.at[side],
-            recv_sem=move_recv.at[side],
-            device_id={"patch": me + step},
-            device_id_type=MESH,
-        )
-
-    for side, step in enumerate((1, -1)):
+                out[place + m] = landing[0, side, m] + (
+                    weights[0] * landing[1, side, m]
+                    + weights[1] * landing[2, side, m]
+                    + weights[2] * landing[3, side, m]
+                )
+
+        @pl.when(jnp.logical_not(exists(-step, 0)))
+        def _():
+            out[pl.ds(place, MOVE_CAP)] = jnp.zeros((MOVE_CAP, species, surface), jnp.float32)
+
         @pl.when(exists(step, 0))
         def _():
-            move(side, step).start()
-
-        @pl.when(jnp.logical_not(exists(-step, 0)))
-        def _():
-            out[pl.ds(slots + side * MOVE_CAP, MOVE_CAP)] = jnp.zeros(
-                (MOVE_CAP, species, surface), jnp.float32
-            )
-
-    for r in range(1, rows + 1):
-        for c in range(1, cols + 1):
-            stays = new_owner(r, c) == me
-            out[(r - 1) * cols + c - 1] = jnp.where(stays, state[r, c], 0.0)
+            for part in range(KRYLOV + 1):
+                move(part, side, step).wait_send()
 
     for at, (dx, dy) in enumerate(DIRECTIONS):
         @pl.when(exists(dx, dy))
         def _():
             for f in range(2):
                 halo(f, at).wait_send()
-
-    for side, step in enumerate((1, -1)):
-        @pl.when(exists(-step, 0))
-        def _():
-            move(side, step).wait_recv()
-
-        @pl.when(exists(step, 0))
-        def _():
-            move(side, step).wait_send()
 
 
 def per_device(owners, bands, previous, predicted, new_owner, levels, diffusion, decay, reaction):
@@ -444,7 +542,10 @@
             pltpu.VMEM((ROWS + 2, cols + 2, 8, surface), jnp.float32),
             pltpu.VMEM((NEWTON, bands, 1, 128), jnp.float32),
             pltpu.VMEM((NEWTON, owners, 1, 128), jnp.float32),
-            pltpu.VMEM((2, MOVE_CAP, species, surface), jnp.float32),
+            pltpu.VMEM((KRYLOV + 1, 2, MOVE_CAP, species, surface), jnp.float32),
+            pltpu.VMEM((KRYLOV + 1, 2, MOVE_CAP, species, surface), jnp.float32),
+            pltpu.VMEM((2, 2, ROWS // 2, species, surface), jnp.float32),
+            pltpu.VMEM((2, 2, ROWS // 2, species, surface), jnp.float32),
             dma((2,)),
             dma((2, len(DIRECTIONS))),
             dma((2, len(DIRECTIONS))),
@@ -452,8 +553,8 @@
             dma((NEWTON, bands)),
             dma((NEWTON, owners)),
             dma((NEWTON, owners)),
-            dma((2,)),
-            dma((2,)),
+            dma((KRYLOV + 1, 2)),
+            dma((KRYLOV + 1, 2)),
         ],
         compiler_params=pltpu.CompilerParams(collective_id=0, has_side_effects=True),
     )(

time: 57.5 us -> 47.1 us (0.82)
  Pallas kernels: 52.9 us -> 42.4 us
    pallas_call x1, Pallas kernels: 52.9 us -> 42.4 us  [per_device(): pl.pallas_call(functools.partial(kernel, owners, bands), out_shape=jax.Sh...]
where the time goes in v2:
time: 47.1 us; the launch traced here: 46.8 us
  Pallas kernels  42.4 us (90%)
  local copies, waits for them, and re-layouts  4.31 us (9%)
    pallas_call x1, Pallas kernels, per_device(): pl.pallas_call(functools.partial(kernel, owners, bands), out_shape=jax.Sh...  42.4 us
    unnamed x4, local copies, waits for them, and re-layouts  2.47 us
    broadcast_in_dim x1, local copies, waits for them, and re-layouts, per_device(): return result[None, None]  1.84 us

profile of v2, /device:TPU:0, one launch (start us, length us, event | category | flops | bytes accessed | tf_op | source)
XLA Modules:
  0.0 46.8 jit_solution(3712208434549071265)
XLA Ops:
  0.0 0.0 copy-start
  0.0 1.7 %copy.10 = f32[1,1,12,21,256]{4,3,1,2,0:T(8,128)} copy(f32[1,1,12,21,256]{4,1,3,2,0:T(1,128)} %param.7) | data formatting | bytes 516096
  1.7 0.0 copy-done
  1.7 0.7 %copy.11 = f32[1,1,12,21,256]{4,3,1,2,0:T(8,128)} copy(f32[1,1,12,21,256]{4,1,3,2,0:T(1,128)S(1)} %copy-done) | data formatting | bytes 516096
  2.5 42.4 %shard_map.73 = f32[16,21,256]{2,1,0:T(8,128)} custom-call(s32[4,8,12]{2,1,0:T(8,128)} %owner_s.1, s32[4,8,12]{2,1,0:T(8,128)} %level_s.1, f32[1,21]{1,0:T(1,128)} %bitcast.8, f32[1,21]{1,0:T(1,128)} %bitcast.9, f32[21,21]{1,0:T(8,128)} %react_in.1, f32[4,3,21,256]{3,2,1,0:T(8,128)} %bitcast.6, f32[4,3,21,256]{3,2,1,0:T(8,128)} %bitcast.7), custom_call_target="tpu_custom_call" | custom-call | tf_op jit(solution)/shard_map/pallas_call | solution.py:535
  44.9 1.8 %copy.9 = f32[1,1,16,21,256]{4,2,3,1,0:T(8,128)} copy(f32[1,1,16,21,256]{4,3,2,1,0:T(8,128)} %bitcast.5) | data formatting | bytes 688128 | tf_op jit(solution)/shard_map/broadcast_in_dim | solution.py:569
Async XLA Ops:
  0.0 1.7 %copy-start = (f32[1,1,12,21,256]{4,1,3,2,0:T(1,128)S(1)}, f32[1,1,12,21,256]{4,1,3,2,0:T(1,128)}, u32[]{:S(2)}) copy-start(f32[1,1,12,21,256]{4,1,3,2,0:T(1,128)} %param.8) | copy-start | bytes 774148

commit v3 on v2

--- a/solution.py
+++ b/solution.py
@@ -102,11 +102,11 @@
 
 def kernel(
     owners, bands, owner_s, level_s, diff_in, decay_in, react_in, prev_in, pred_in, out,
-    state, before, k0, k1, k2, k3, face, gram_a, gram_b, movers, landing, strip_out, strip_in,
+    state, before, k0, k1, k2, k3, face, gram_a, gram_b, movers, landing, strip_out, strip_in, stage,
     local_sem, halo_send, halo_recv, a_send, a_recv, b_send, b_recv, move_send, move_recv,
 ):
-    rows, cols, species, surface = prev_in.shape
-    ext_rows, ext_cols = rows + 2, cols + 2
+    ext_rows, ext_cols, species, surface = state.shape
+    rows, cols = ext_rows - 2, ext_cols - 2
     me = lax.axis_index("patch")
     band = lax.axis_index("grp")
     MESH = pl.DeviceIdType.MESH
@@ -142,9 +142,7 @@
 
     fields = ((pred_in, state), (prev_in, before))
     own = [
-        pltpu.make_async_copy(
-            src, dst.at[pl.ds(1, rows), pl.ds(1, cols)], local_sem.at[f]
-        )
+        pltpu.make_async_copy(src, stage.at[f], local_sem.at[f])
         for f, (src, dst) in enumerate(fields)
     ]
     for copy in own:
@@ -156,14 +154,14 @@
 
     def span(delta, length):
         if delta == 0:
-            return pl.ds(0, length), pl.ds(1, length)
+            return pl.ds(1, length), pl.ds(1, length)
         if delta > 0:
-            return pl.ds(length - 1, 1), pl.ds(0, 1)
-        return pl.ds(0, 1), pl.ds(length + 1, 1)
+            return pl.ds(length, 1), pl.ds(0, 1)
+        return pl.ds(1, 1), pl.ds(length + 1, 1)
 
     def halo(f, at):
         dx, dy = DIRECTIONS[at]
-        src, dst = fields[f]
+        field = fields[f][1]
         if dy == 0:
             side = 0 if dx > 0 else 1
             source, target = strip_out.at[f, side], strip_in.at[f, side]
@@ -171,8 +169,8 @@
             lanes = high if dy > 0 else low
             col_from, col_to = span(dx, cols)
             row_from, row_to = span(dy, rows)
-            source = src.at[row_from, col_from, :, lanes]
-            target = dst.at[row_to, col_to, :, lanes]
+            source = field.at[row_from, col_from, :, lanes]
+            target = field.at[row_to, col_to, :, lanes]
         return pltpu.make_async_remote_copy(
             src_ref=source,
             dst_ref=target,
@@ -186,10 +184,16 @@
     cell_col, cell_row = lane % CELLS, lane // CELLS
     right_half = cell_col >= CELLS // 2
 
-    for copy in own:
-        copy.wait()
     for f in range(2):
+        own[f].wait()
         field = fields[f][1]
+        for r in range(rows):
+            for c in range(cols):
+                for part, lanes in enumerate((low, high)):
+                    first = (r * cols + c) * species * 2 + part
+                    field[r + 1, c + 1, :, lanes] = stage[
+                        f, pl.ds(first, species, stride=2), :
+                    ]
         for k in range(pairs):
             first, second = field[2 * k + 1, cols], field[2 * k + 2, cols]
             strip_out[f, 0, k] = jnp.where(
@@ -208,8 +212,7 @@
     for at, (dx, dy) in enumerate(DIRECTIONS):
         @pl.when(exists(dx, dy))
         def _():
-            for f in range(2):
-                halo(f, at).start()
+            halo(0, at).start()
 
         @pl.when(jnp.logical_not(exists(-dx, -dy)))
         def _():
@@ -218,6 +221,11 @@
             shape = (row_to.size, col_to.size, species, lanes.size)
             for f in range(2):
                 fields[f][1][row_to, col_to, :, lanes] = jnp.zeros(shape, jnp.float32)
+
+    for at, (dx, dy) in enumerate(DIRECTIONS):
+        @pl.when(exists(dx, dy))
+        def _():
+            halo(1, at).start()
 
     west_edge, east_edge = cell_col == 0, cell_col == CELLS - 1
     south_edge, north_edge = cell_row == 0, cell_row == CELLS - 1
@@ -255,13 +263,12 @@
                 face[r, c, pl.ds(d, 1), :] = value
             face[r, c, pl.ds(4, 1), :] = west + east + south + north
 
-    for at, (dx, dy) in enumerate(DIRECTIONS):
-        @pl.when(exists(-dx, -dy))
-        def _():
-            for f in range(2):
+    def receive(f):
+        for at, (dx, dy) in enumerate(DIRECTIONS):
+            @pl.when(exists(-dx, -dy))
+            def _():
                 halo(f, at).wait_recv()
-            if dy == 0:
-                for f in range(2):
+                if dy == 0:
                     for k in range(pairs):
                         strip = strip_in[f, 0 if dx > 0 else 1, k]
                         at_col = 0 if dx > 0 else cols + 1
@@ -314,8 +321,10 @@
 
     full = pl.ds(0, surface)
 
-    def sweep(src, dst, finish, ring):
-        col_from, col_to = (0, ext_cols) if ring else (1, cols + 1)
+    def sweep(src, dst, finish, own=True, ring=True):
+        columns = list(range(1, cols + 1)) if own else []
+        if ring:
+            columns = [0, *columns, cols + 1]
 
         def masked(r, c, lanes, x, lap):
             return finish(r, c, lanes, x, lap) * inside(r, c)
@@ -328,7 +337,7 @@
 
         @pl.loop(1, rows + 1)
         def _(r):
-            for c in range(col_from, col_to):
+            for c in columns:
                 patch(
                     src, dst, masked if c in (0, cols + 1) else finish,
                     r, c, full, (r - 1, full), (r + 1, full),
@@ -364,6 +373,13 @@
         return owner_s[band, me, (r - 1) * cols + c - 1]
 
     slots = rows * cols
+
+    def emit(slot, value):
+        for part in range(2):
+            first = slot // 8 * 16 + part * 8 + slot % 8
+            out[pl.ds(first, species, stride=2 * (slots + 2 * MOVE_CAP)), :] = (
+                value[:, part * half : (part + 1) * half]
+            )
 
     def move(part, side, step):
         return pltpu.make_async_remote_copy(
@@ -395,21 +411,32 @@
         final = newton_step == NEWTON - 1
         if final:
             send_movers(0, state)
-        sweep(state, k0, residual, True)
+        if newton_step == 0:
+            receive(0)
+            sweep(state, k0, residual, ring=False)
+            receive(1)
+            sweep(state, k0, residual, own=False)
+        else:
+            sweep(state, k0, residual)
         for j in range(KRYLOV):
             if final:
                 send_movers(j + 1, krylov[j])
-            sweep(krylov[j], krylov[j + 1], jacobian, j < KRYLOV - 1)
+            sweep(krylov[j], krylov[j + 1], jacobian, ring=j < KRYLOV - 1)
+        def products(r, sums):
+            for c in range(1, cols + 1):
+                values = [field[r, c] for field in krylov]
+                new = []
+                for (i, j), acc in zip(PAIRS, sums):
+                    value = values[i] * values[j]
+                    new.append(acc + (value[:, :half] + value[:, half:]))
+                sums = tuple(new)
+            return sums
+
+        sums = lax.fori_loop(
+            1, rows + 1, products, tuple(jnp.zeros((species, half), jnp.float32) for _ in PAIRS)
+        )
         line = jnp.zeros((1, 128), jnp.float32)
-        for at, (i, j) in enumerate(PAIRS):
-            def products(r, acc, i=i, j=j):
-                for c in range(1, cols + 1):
-                    acc = acc + krylov[i][r, c] * krylov[j][r, c]
-                return acc
-
-            acc = lax.fori_loop(
-                1, rows + 1, products, jnp.zeros((species, surface), jnp.float32)
-            )
+        for at, acc in enumerate(sums):
             value = jnp.sum(jnp.sum(acc, axis=0, keepdims=True), axis=1, keepdims=True)
             line = line + jnp.where(out_lane == at, value, 0.0)
 
@@ -470,6 +497,13 @@
                 + weights[2][:, : lanes.size] * k2[r, c, :, lanes]
             )
 
+        if newton_step == 0:
+            for at, (dx, dy) in enumerate(DIRECTIONS):
+                @pl.when(exists(dx, dy))
+                def _():
+                    for f in range(2):
+                        halo(f, at).wait_send()
+
         if not final:
             for c in range(ext_cols):
                 state[0, c, :, high] = update(0, c, high)
@@ -480,11 +514,12 @@
                 for c in range(ext_cols):
                     state[r, c] = update(r, c, full)
         else:
-            @pl.loop(1, rows + 1)
-            def _(r):
+            for r in range(1, rows + 1):
                 for c in range(1, cols + 1):
                     stays = new_owner(r, c) == me
-                    out[(r - 1) * cols + c - 1] = jnp.where(stays, update(r, c, full), 0.0)
+                    emit(
+                        (r - 1) * cols + c - 1, jnp.where(stays, update(r, c, full), 0.0)
+                    )
 
         for d in range(1, bands):
             send_a(d, band, band).wait_send()
@@ -501,40 +536,36 @@
             for part in range(KRYLOV + 1):
                 move(part, side, step).wait_recv()
             for m in range(MOVE_CAP):
-                out[place + m] = landing[0, side, m] + (
+                emit(place + m, landing[0, side, m] + (
                     weights[0] * landing[1, side, m]
                     + weights[1] * landing[2, side, m]
                     + weights[2] * landing[3, side, m]
-                )
+                ))
 
         @pl.when(jnp.logical_not(exists(-step, 0)))
         def _():
-            out[pl.ds(place, MOVE_CAP)] = jnp.zeros((MOVE_CAP, species, surface), jnp.float32)
+            for m in range(MOVE_CAP):
+                emit(place + m, jnp.zeros((species, surface), jnp.float32))
 
         @pl.when(exists(step, 0))
         def _():
             for part in range(KRYLOV + 1):
                 move(part, side, step).wait_send()
 
-    for at, (dx, dy) in enumerate(DIRECTIONS):
-        @pl.when(exists(dx, dy))
-        def _():
-            for f in range(2):
-                halo(f, at).wait_send()
-
 
 def per_device(owners, bands, previous, predicted, new_owner, levels, diffusion, decay, reaction):
     patches, species, surface = previous.shape[2:]
     cols = patches // ROWS
     ext = (ROWS + 2, cols + 2, species, surface)
-    grid = (ROWS, cols, species, surface)
+    linear = (patches * species * 2, surface // 2)
+    slots = patches + 2 * MOVE_CAP
     vmem = pl.BlockSpec(memory_space=pltpu.VMEM)
     smem = pl.BlockSpec(memory_space=pltpu.SMEM)
     anywhere = pl.BlockSpec(memory_space=pl.ANY)
     dma = pltpu.SemaphoreType.DMA
     result = pl.pallas_call(
         functools.partial(kernel, owners, bands),
-        out_shape=jax.ShapeDtypeStruct((patches + 2 * MOVE_CAP, species, surface), jnp.float32),
+        out_shape=jax.ShapeDtypeStruct((species * slots * 2, surface // 2), jnp.float32),
         in_specs=[smem, smem, vmem, vmem, vmem, anywhere, anywhere],
         out_specs=vmem,
         scratch_shapes=[
@@ -546,6 +577,7 @@
             pltpu.VMEM((KRYLOV + 1, 2, MOVE_CAP, species, surface), jnp.float32),
             pltpu.VMEM((2, 2, ROWS // 2, species, surface), jnp.float32),
             pltpu.VMEM((2, 2, ROWS // 2, species, surface), jnp.float32),
+            pltpu.VMEM((2, *linear), jnp.float32),
             dma((2,)),
             dma((2, len(DIRECTIONS))),
             dma((2, len(DIRECTIONS))),
@@ -563,10 +595,11 @@
         diffusion.reshape(1, species),
         decay.reshape(1, species),
         reaction,
-        previous.reshape(grid),
-        predicted.reshape(grid),
+        previous.reshape(linear),
+        predicted.reshape(linear),
     )
-    return result[None, None]
+    result = result.reshape(species, slots // 8, 2, 8, surface // 2)
+    return result.transpose(1, 3, 0, 2, 4).reshape(1, 1, slots, species, surface)
 
 
 def solution(mesh):

time: 47.1 us -> 42.4 us (0.900)
  local copies, waits for them, and re-layouts: 4.31 us -> 1.73 us
  Pallas kernels: 42.4 us -> 40.4 us
    pallas_call x1, Pallas kernels: 42.4 us -> 40.4 us  [per_device(): pl.pallas_call(functools.partial(kernel, owners, bands), out_shape=jax.Sh...]
    broadcast_in_dim x1 -> x0, local copies, waits for them, and re-layouts: 1.84 us -> none  [per_device(): return result[None, None]]
    unnamed x4 -> x1, local copies, waits for them, and re-layouts: 2.47 us -> 1.73 us
where the time goes in v3:
time: 42.4 us; the launch traced here: 42.2 us
  Pallas kernels  40.4 us (95%)
  local copies, waits for them, and re-layouts  1.73 us (4%)
    pallas_call x1, Pallas kernels, per_device(): pl.pallas_call(functools.partial(kernel, owners, bands), out_shape=jax.Sh...  40.4 us
    unnamed x1, local copies, waits for them, and re-layouts  1.73 us

profile of v3, /device:TPU:0, one launch (start us, length us, event | category | flops | bytes accessed | tf_op | source)
XLA Modules:
  0.0 42.2 jit_solution(8150466660844088201)
XLA Ops:
  0.0 40.4 %shard_map.73 = f32[672,128]{1,0:T(8,128)} custom-call(s32[4,8,12]{2,1,0:T(8,128)} %owner_s.1, s32[4,8,12]{2,1,0:T(8,128)} %level_s.1, f32[1,21]{1,0:T(1,128)} %bitcast.12, f32[1,21]{1,0:T(1,128)} %bitcast.13, f32[21,21]{1,0:T(8,128)} %react_in.1, f32[504,128]{1,0:T(8,128)} %bitcast.10, f32[504,128]{1,0:T(8,128)} %bitcast.11), custom_call_target="tpu_custom_call" | custom-call | tf_op jit(solution)/shard_map/pallas_call | solution.py:566
  40.4 1.7 %copy.9 = f32[1,1,16,21,256]{4,2,3,1,0:T(8,128)} copy(f32[1,1,16,21,256]{4,2,3,1,0:T(8,128)} %bitcast.9) | data formatting | bytes 688128

commit v4 on v3

--- a/solution.py
+++ b/solution.py
@@ -15,11 +15,10 @@
 
 step_rate = 4.0
 epsilon = 1e-12
-highest = lax.Precision.HIGHEST
 SHIFT = 16.0
 SCALE = 64.0
 PAIRS = [(i, j) for j in range(KRYLOV + 1) for i in range(j + 1)]
-DIRECTIONS = [(x, y) for x in (-1, 0, 1) for y in (-1, 0, 1) if (x, y) != (0, 0)]
+DIRECTIONS = [(1, 0), (-1, 0), (1, 1), (-1, -1), (1, -1), (-1, 1), (0, 1), (0, -1)]
 
 
 def small_solve(matrix, vector):
@@ -335,7 +334,7 @@
                 patch(src, dst, masked, 0, c, high, None, (1, low))
                 patch(src, dst, masked, last, c, low, (last - 1, high), None)
 
-        @pl.loop(1, rows + 1)
+        @pl.loop(1, rows + 1, unroll=True)
         def _(r):
             for c in columns:
                 patch(
@@ -347,9 +346,10 @@
         big = value.astype(jnp.bfloat16)
         return big, (value - big.astype(jnp.float32)).astype(jnp.bfloat16)
 
-    react_big, react_small = split(reaction_a)
-
-    def mixing(x):
+    react_parts, react_a_parts = split(reaction), split(reaction_a)
+
+    def mixing(parts, x):
+        react_big, react_small = parts
         big, small = split(x)
 
         def product(a, b):
@@ -358,13 +358,12 @@
         return product(react_small, big) + product(react_big, small) + product(react_big, big)
 
     def residual(r, c, lanes, x, lap):
-        mixed = jnp.dot(reaction, x, precision=highest, preferred_element_type=jnp.float32)
         old = before[r, c, :, lanes]
-        return rate * (x - old) - diffusion * lap - mixed + decay * (x * x * x)
+        return rate * (x - old) - diffusion * lap - mixing(react_parts, x) + decay * (x * x * x)
 
     def jacobian(r, c, lanes, x, lap):
         u = state[r, c, :, lanes]
-        return (rate_a + decay_a * (u * u)) * x - diffusion_a * lap - mixing(x)
+        return (rate_a + decay_a * (u * u)) * x - diffusion_a * lap - mixing(react_a_parts, x)
 
     krylov = (k0, k1, k2, k3)
     out_lane = lax.broadcasted_iota(jnp.int32, (1, 128), 1)

time: 42.4 us -> 39.6 us (0.934)
  Pallas kernels: 40.4 us -> 37.6 us
    pallas_call x1, Pallas kernels: 40.4 us -> 37.6 us  [per_device(): pl.pallas_call(functools.partial(kernel, owners, bands), out_shape=jax.Sh...]
where the time goes in v4:
time: 39.6 us; the launch traced here: 39.3 us
  Pallas kernels  37.6 us (95%)
  local copies, waits for them, and re-layouts  1.73 us (4%)
    pallas_call x1, Pallas kernels, per_device(): pl.pallas_call(functools.partial(kernel, owners, bands), out_shape=jax.Sh...  37.6 us
    unnamed x1, local copies, waits for them, and re-layouts  1.73 us

profile of v4, /device:TPU:0, one launch (start us, length us, event | category | flops | bytes accessed | tf_op | source)
XLA Modules:
  0.0 39.3 jit_solution(9317682855396244950)
XLA Ops:
  0.0 37.6 %shard_map.73 = f32[672,128]{1,0:T(8,128)} custom-call(s32[4,8,12]{2,1,0:T(8,128)} %owner_s.1, s32[4,8,12]{2,1,0:T(8,128)} %level_s.1, f32[1,21]{1,0:T(1,128)} %bitcast.12, f32[1,21]{1,0:T(1,128)} %bitcast.13, f32[21,21]{1,0:T(8,128)} %react_in.1, f32[504,128]{1,0:T(8,128)} %bitcast.10, f32[504,128]{1,0:T(8,128)} %bitcast.11), custom_call_target="tpu_custom_call" | custom-call | tf_op jit(solution)/shard_map/pallas_call | solution.py:565
  37.6 1.7 %copy.9 = f32[1,1,16,21,256]{4,2,3,1,0:T(8,128)} copy(f32[1,1,16,21,256]{4,2,3,1,0:T(8,128)} %bitcast.9) | data formatting | bytes 688128
